TPU v7x, 128 devices: a whole 4x4x4 slice. The times are simulated.
128 devices in a mesh: neuron: 16 (over z, y), trial: 8 (over x, core).
Axes of the slice: x: 4, y: 4, z: 4, core: 2. Of those that a mesh axis runs over, the one named last changes fastest.
Arguments:
- drive: bfloat16 [8, 128, 131072], P(None, 'trial', 'neuron'), may hold values from -6 to 6
- learning: bfloat16 [8, 128, 131072], P(None, 'trial', 'neuron'), may hold values from -6 to 6
- membrane_init: float32 [128, 131072], P('trial', 'neuron'), may hold values from -3 to 3
- adapt_init: float32 [128, 131072], P('trial', 'neuron'), may hold values from 0 to 1
- trace_init: float32 [128, 131072], P('trial', 'neuron'), may hold values from 0 to 3
- membrane_decay: float32 [131072], P('neuron'), may hold values from 0.6 to 0.95
- adapt_decay: float32 [131072], P('neuron'), may hold values from 0.8 to 0.99
- adapt_gain: float32 [131072], P('neuron'), may hold values from 0.2 to 1
- threshold: float32 [131072], P('neuron'), may hold values from 0.5 to 1.5
- left_factor: bfloat16 [131072, 512], P('neuron'), may hold values from -6 to 6
- right_factor: bfloat16 [131072, 512], P('neuron'), may hold values from -16 to 16
Outputs:
- left_new: bfloat16 [131072, 512], P(('neuron', 'trial'))
- right_new: bfloat16 [131072, 512], P(('neuron', 'trial'))
All inputs are finite; a program needn't handle non-finite values.
Results may differ from a plain program's by a relative error of at most 0.0085.
Values may be sent and summed in bfloat16 or wider, within the bound.
No kernel may reach another device: no remote copies, remote signals or barrier semaphores. Data moves between devices by JAX's collectives and lax.ppermute only.
A program may use at most 128 MiB of HBM per device.

v0:
```python
import math
import jax
import jax.numpy as jnp
from jax import lax
from jax.sharding import PartitionSpec as P

sharpness = 3.0
learn_rate = 0.5


def rank_block(values, factor, weight):
    return jnp.dot(values, factor, preferred_element_type=jnp.float32) * weight


def shards(
    drive,
    learning,
    membrane_init,
    adapt_init,
    trace_init,
    membrane_decay,
    adapt_decay,
    adapt_gain,
    threshold,
    left_factor,
    right_factor,
):
    local_neurons = left_factor.shape[0]
    rank_width = left_factor.shape[1]
    step_count = drive.shape[0]
    neuron_count = local_neurons * lax.axis_size("neuron")
    norm_neurons = 1.0 / math.sqrt(neuron_count)
    norm_rank = 1.0 / math.sqrt(rank_width)
    membrane = membrane_init
    adaptation = adapt_init
    filtered = trace_init
    spikes = jax.nn.sigmoid(sharpness * (membrane - threshold - adapt_gain * adaptation))
    signals = []
    presyns = []
    g_blocks = []
    k_blocks = []
    for moment in range(step_count):
        partial_value = rank_block(spikes.astype(jnp.bfloat16), right_factor, norm_neurons)
        projected = lax.psum(partial_value, "neuron").astype(jnp.bfloat16)
        current = (
            lax.dot_general(
                projected, left_factor, (((1,), (1,)), ((), ())), preferred_element_type=jnp.float32
            )
            * norm_rank
        )
        membrane = (
            membrane_decay * membrane
            + drive[moment].astype(jnp.float32)
            + current
            - threshold * spikes
        )
        adaptation = adapt_decay * adaptation + spikes
        spikes = jax.nn.sigmoid(sharpness * (membrane - threshold - adapt_gain * adaptation))
        slope_value = sharpness * spikes * (1.0 - spikes)
        filtered = membrane_decay * filtered + spikes
        signal = (learning[moment].astype(jnp.float32) * slope_value).astype(jnp.bfloat16)
        presyn = filtered.astype(jnp.bfloat16)
        signals.append(signal)
        presyns.append(presyn)
        g_part = rank_block(presyn, right_factor, norm_neurons)
        k_part = rank_block(signal, left_factor, norm_neurons)
        g_total, k_total = lax.psum((g_part, k_part), "neuron")
        g_blocks.append(g_total.astype(jnp.bfloat16))
        k_blocks.append(k_total.astype(jnp.bfloat16))
    signal_all = jnp.stack(signals)
    presyn_all = jnp.stack(presyns)
    rank_g = jnp.stack(g_blocks)
    rank_k = jnp.stack(k_blocks)
    stored = local_neurons // lax.axis_size("trial")
    offset = lax.axis_index("trial") * stored
    left_rows = lax.dynamic_slice_in_dim(left_factor, offset, stored, 0).astype(jnp.float32)
    right_rows = lax.dynamic_slice_in_dim(right_factor, offset, stored, 0).astype(jnp.float32)
    contract_lead = (((0, 1), (0, 1)), ((), ()))
    signal_mine, presyn_mine = (
        lax.all_to_all(signal_all, "trial", split_axis=2, concat_axis=1, tiled=True),
        lax.all_to_all(presyn_all, "trial", split_axis=2, concat_axis=1, tiled=True),
    )
    first = lax.dot_general(
        signal_mine,
        lax.all_gather(rank_g, "trial", axis=1, tiled=True),
        contract_lead,
        preferred_element_type=jnp.float32,
    )
    second = lax.dot_general(
        presyn_mine,
        lax.all_gather(rank_k, "trial", axis=1, tiled=True),
        contract_lead,
        preferred_element_type=jnp.float32,
    )
    left_step = left_rows - learn_rate * (first * norm_rank)
    right_step = right_rows - learn_rate * (second * norm_rank)
    highest = lax.Precision.HIGHEST
    row_lead = (((0,), (0,)), ((), ()))
    gram_one = lax.psum(
        lax.dot_general(right_step, right_step, row_lead, precision=highest), ("neuron", "trial")
    )
    lower_one = jnp.linalg.cholesky(gram_one)
    basis = lax.linalg.triangular_solve(
        lower_one, right_step, left_side=False, lower=True, transpose_a=True
    )
    right_new = (basis * math.sqrt(neuron_count)).astype(jnp.bfloat16)
    left_new = (jnp.dot(left_step, lower_one, precision=highest) * norm_neurons).astype(
        jnp.bfloat16
    )
    return (left_new, right_new)


def solution(mesh):
    in_specs = (
        P(None, "trial", "neuron"),
        P(None, "trial", "neuron"),
        P("trial", "neuron"),
        P("trial", "neuron"),
        P("trial", "neuron"),
        P("neuron"),
        P("neuron"),
        P("neuron"),
        P("neuron"),
        P("neuron", None),
        P("neuron", None),
    )
    out_specs = (P(("neuron", "trial"), None), P(("neuron", "trial"), None))
    return jax.shard_map(shards, mesh=mesh, in_specs=in_specs, out_specs=out_specs, check_vma=False)
```

profile of v0, /device:TPU:1, one launch (start us, length us, event | category | flops | bytes accessed | tf_op | source)
XLA Modules:
  0.0 1214.8 jit_solution(1713676997602515515)
XLA Ops:
  7.3 5.0 convolution_multiply_fusion.31
  12.3 62.5 %psum.175 = bf16[16,512]{1,0:T(8,128)(2,1)S(1)} all-reduce(f32[16,512]{1,0:T(8,128)S(1)} %convolution_multiply_fusion.31), channel_id=1, replica_groups=mesh['neuron'=16,'trial'=8] {'neuron'}, use_global_device_ids=true, to_apply=%region_0.0 | all-reduce | flops 8192 | bytes 49152 | tf_op jit(solution)/shard_map/psum | solution.py:44
  74.9 6.7 bitcast_dynamic-update-slice_fusion.8
  82.8 55.9 %psum.176 = bf16[16,512]{1,0:T(8,128)(2,1)S(1)} all-reduce(f32[16,512]{1,0:T(8,128)S(1)} %convolution_multiply_fusion.30), channel_id=1, replica_groups=mesh['neuron'=16,'trial'=8] {'neuron'}, use_global_device_ids=true, to_apply=%region_1.0 | all-reduce | flops 8192 | bytes 49152 | tf_op jit(solution)/shard_map/psum | solution.py:44
  138.7 7.0 bitcast_dynamic-update-slice_fusion.7
  145.7 5.0 convolution_multiply_fusion.29
  150.7 56.0 %psum.177 = bf16[16,512]{1,0:T(8,128)(2,1)S(1)} all-reduce(f32[16,512]{1,0:T(8,128)S(1)} %convolution_multiply_fusion.29), channel_id=1, replica_groups=mesh['neuron'=16,'trial'=8] {'neuron'}, use_global_device_ids=true, to_apply=%region_2.0 | all-reduce | flops 8192 | bytes 49152 | tf_op jit(solution)/shard_map/psum | solution.py:44
  206.6 6.7 bitcast_dynamic-update-slice_fusion.6
  213.3 4.6 convolution_multiply_fusion.28
  217.9 55.9 %psum.178 = bf16[16,512]{1,0:T(8,128)(2,1)S(1)} all-reduce(f32[16,512]{1,0:T(8,128)S(1)} %convolution_multiply_fusion.28), channel_id=1, replica_groups=mesh['neuron'=16,'trial'=8] {'neuron'}, use_global_device_ids=true, to_apply=%region_3.0 | all-reduce | flops 8192 | bytes 49152 | tf_op jit(solution)/shard_map/psum | solution.py:44
  273.7 7.1 bitcast_dynamic-update-slice_fusion.5
  282.6 4.6 convolution_multiply_fusion.27
  287.2 56.4 %psum.179 = bf16[16,512]{1,0:T(8,128)(2,1)S(1)} all-reduce(f32[16,512]{1,0:T(8,128)S(1)} %convolution_multiply_fusion.27), channel_id=1, replica_groups=mesh['neuron'=16,'trial'=8] {'neuron'}, use_global_device_ids=true, to_apply=%region_4.0 | all-reduce | flops 8192 | bytes 49152 | tf_op jit(solution)/shard_map/psum | solution.py:44
  343.6 7.0 bitcast_dynamic-update-slice_fusion.4
  350.6 4.6 convolution_multiply_fusion.26
  355.2 55.7 %psum.180 = bf16[16,512]{1,0:T(8,128)(2,1)S(1)} all-reduce(f32[16,512]{1,0:T(8,128)S(1)} %convolution_multiply_fusion.26), channel_id=1, replica_groups=mesh['neuron'=16,'trial'=8] {'neuron'}, use_global_device_ids=true, to_apply=%region_5.0 | all-reduce | flops 8192 | bytes 49152 | tf_op jit(solution)/shard_map/psum | solution.py:44
  410.9 7.4 bitcast_dynamic-update-slice_fusion.3
  420.1 5.2 convolution_multiply_fusion.25
  425.3 56.5 %psum.181 = bf16[16,512]{1,0:T(8,128)(2,1)S(1)} all-reduce(f32[16,512]{1,0:T(8,128)} %convolution_multiply_fusion.25), channel_id=1, replica_groups=mesh['neuron'=16,'trial'=8] {'neuron'}, use_global_device_ids=true, to_apply=%region_6.0 | all-reduce | flops 8192 | bytes 49152 | tf_op jit(solution)/shard_map/psum | solution.py:44
  481.7 7.4 bitcast_dynamic-update-slice_fusion.2
  489.1 5.4 convolution_multiply_fusion.24
  494.5 5.3 convolution_multiply_fusion.9
  516.7 55.9 %psum.182 = bf16[16,512]{1,0:T(8,128)(2,1)S(1)} all-reduce(f32[16,512]{1,0:T(8,128)S(1)} %copy-done.39), channel_id=1, replica_groups=mesh['neuron'=16,'trial'=8] {'neuron'}, use_global_device_ids=true, to_apply=%region_7.0 | all-reduce | flops 8192 | bytes 49152 | tf_op jit(solution)/shard_map/psum | solution.py:44
  572.7 6.6 bitcast_dynamic-update-slice_fusion.1
  579.3 4.8 convolution_multiply_fusion.8
  584.1 4.7 convolution_multiply_fusion.16
  593.8 61.6 %all-reduce.6 = (bf16[16,512]{1,0:T(8,128)(2,1)S(1)}, bf16[16,512]{1,0:T(8,128)(2,1)S(1)}, bf16[16,512]{1,0:T(8,128)(2,1)S(1)}, bf16[16,512]{1,0:T(8,128)(2,1)S(...) all-reduce(f32[16,512]{1,0:T(8,128)S(1)} %convolution_multiply_fusi, ...), channel_id=1, replica_groups=mesh['neuron'=16,'trial'=8] {'neuron'}, use_global_device_ids=true, to_apply=%region_8.0 | all-reduce | flops 131072 | bytes 786432 | tf_op jit(solution)/shard_map/psum | solution.py:67
  656.1 13.1 %copy.34 = bf16[8,16,8192]{1,0,2:T(8,128)(2,1)} copy(bf16[8,16,8192]{2,1,0:T(8,128)(2,1)S(1)} %copy-done.19) | data formatting | bytes 4194304 | tf_op jit(solution)/shard_map/stack | solution.py:71
  669.3 19.6 %reshape.114 = bf16[8,2,65536]{2,1,0:T(2,128)(2,1)} reshape(bf16[8192,8,16]{2,1,0:T(8,128)(2,1)} %bitcast.266) | data formatting | bytes 4194304
  688.8 128.3 %all-to-all-start.1 = ((bf16[8,2,65536]{2,1,0:T(2,128)(2,1)}), bf16[8,2,65536]{2,1,0:T(2,128)(2,1)S(1)}, u32[]{:S(2)}, u32[]{:S(2)}) async-start(bf16[8,2,65536]{2,1,0:T(2,128)(2,1)} %reshape.114), calls=%async_computation.1 | async-start | bytes 4194304 | tf_op jit(solution)/shard_map/all_to_all | solution.py:81
  819.8 14.5 %copy.30 = bf16[8,16,8192]{1,0,2:T(8,128)(2,1)} copy(bf16[8,16,8192]{2,1,0:T(8,128)(2,1)} %bitcast_dynamic-update-slice_fusion.9) | data formatting | bytes 4194304 | tf_op jit(solution)/shard_map/stack | solution.py:70
  834.4 19.6 %reshape.112 = bf16[8,2,65536]{2,1,0:T(2,128)(2,1)} reshape(bf16[8192,8,16]{2,1,0:T(8,128)(2,1)} %bitcast.267) | data formatting | bytes 4194304
  853.9 4.8 all-to-all-start
  858.7 13.1 %reshape.115 = bf16[8192,8,16]{2,1,0:T(8,128)(2,1)} reshape(bf16[8,2,65536]{2,1,0:T(2,128)(2,1)S(1)} %all-to-all-done.1) | data formatting | bytes 4194304
  871.8 17.1 %copy.36 = bf16[8,8,16,1024]{3,2,1,0:T(8,128)(2,1)} copy(bf16[8,8,16,1024]{2,0,3,1:T(8,128)(2,1)} %bitcast.268) | data formatting | bytes 4194304 | tf_op jit(solution)/shard_map/all_to_all | solution.py:81
  896.9 13.9 %reshape.113 = bf16[8192,8,16]{2,1,0:T(8,128)(2,1)} reshape(bf16[8,2,65536]{2,1,0:T(2,128)(2,1)} %all-to-all-done) | data formatting | bytes 4194304
  910.8 17.5 %copy.32 = bf16[8,8,16,1024]{3,2,1,0:T(8,128)(2,1)} copy(bf16[8,8,16,1024]{2,0,3,1:T(8,128)(2,1)} %bitcast.269) | data formatting | bytes 4194304 | tf_op jit(solution)/shard_map/all_to_all | solution.py:80
  932.8 109.1 %all-reduce.5.cloned.1.call-done = f32[512,512]{0,1:T(8,128)} async-done(((f32[512,512]{0,1:T(8,128)}), f32[512,512]{0,1:T(8,128)}) %all-reduce.5.cloned.1.call-update) | async-done | bytes 1048592 | tf_op jit(solution)/shard_map/psum | solution.py:99
  1047.0 11.7 cholesky.104
  1058.9 9.8 custom-call.30
  1071.2 11.7 cholesky.217
  1083.0 9.9 custom-call.31
  1094.5 11.7 cholesky.238
  1106.9 9.8 custom-call.32
  1118.1 11.9 cholesky.255
  1135.0 13.6 %while.1 = (s32[]{:T(128)}, f32[512,512]{1,0:T(8,128)}, s32[4,2]{0,1:T(2,128)S(1)}, f32[4,128,128]{2,1,0:T(8,128)}, s32[]{:T(128)}) while((s32[]{:T(128)}, f32[512,512]{1,0:T(8,128)}, s32[4,2]{0,1:T(2,128)S(1)}, f32[4,128,128]{2,1,0:T(8,128)}, s32[]{:T(128)}) %tuple.66), condition=%wide.while_cond, body=%wide.while_body.sunk | while | flops 2 | bytes 132705 | solution.py:103
  1148.7 40.1 %custom-call.33 = f32[4,128,128]{1,2,0:T(8,128)S(1)} custom-call(f32[4,128,128]{2,1,0:T(8,128)} %get-tuple-element.9), custom_call_target="InvertDiagBlocksLowerTriangular" | custom-call | tf_op jit(solution)/shard_map/triangular_solve | solution.py:103
  1201.5 6.4 multiply_convert_fusion
  (185 shorter events, 82.4 us)
Async XLA Ops:
  7.2 67.7 %copy-start.11 = (f32[16,8192]{1,0:T(8,128)S(1)}, f32[16,8192]{1,0:T(8,128)}, u32[]{:S(2)}) copy-start(f32[16,8192]{1,0:T(8,128)} %param.13) | copy-start | bytes 1572868
  7.2 67.7 %copy-start.10 = (f32[16,8192]{1,0:T(8,128)S(1)}, f32[16,8192]{1,0:T(8,128)}, u32[]{:S(2)}) copy-start(f32[16,8192]{1,0:T(8,128)} %param.14) | copy-start | bytes 1572868
  7.2 67.7 %copy-start.17 = (f32[8192]{0:T(1024)S(1)}, f32[8192]{0:T(1024)}, u32[]{:S(2)}) copy-start(f32[8192]{0:T(1024)} %param.18) | copy-start | bytes 98308
  7.2 67.6 %copy-start.18 = (f32[8192]{0:T(1024)S(1)}, f32[8192]{0:T(1024)}, u32[]{:S(2)}) copy-start(f32[8192]{0:T(1024)} %param.19) | copy-start | bytes 98308
  7.2 67.6 %copy-start.25 = (f32[16,8192]{1,0:T(8,128)S(1)}, f32[16,8192]{1,0:T(8,128)}, u32[]{:S(2)}) copy-start(f32[16,8192]{1,0:T(8,128)} %param.15) | copy-start | bytes 1572868
  7.2 67.6 %copy-start.23 = (f32[8192]{0:T(1024)S(1)}, f32[8192]{0:T(1024)}, u32[]{:S(2)}) copy-start(f32[8192]{0:T(1024)} %param.16) | copy-start | bytes 98308
  7.2 67.6 %copy-start.24 = (f32[8192]{0:T(1024)S(1)}, f32[8192]{0:T(1024)}, u32[]{:S(2)}) copy-start(f32[8192]{0:T(1024)} %param.17) | copy-start | bytes 98308
  7.2 881.6 %all-gather.5.cloned.1.call-start = ((), (), s32[]{:S(2)}) async-start(), calls=%async_computation.3 | async-start | bytes 1179648 | tf_op jit(solution)/shard_map/all_gather | solution.py:91
  74.9 6.7 copy-start
  145.7 60.9 %copy-start.13 = (f32[16,8192]{1,0:T(8,128)}, f32[16,8192]{1,0:T(8,128)S(1)}, u32[]{:S(2)}) copy-start(f32[16,8192]{1,0:T(8,128)S(1)} %get-tuple-element.64) | copy-start | bytes 1572868
  145.7 128.1 %copy-start.2 = (f32[16,8192]{1,0:T(8,128)}, f32[16,8192]{1,0:T(8,128)S(1)}, u32[]{:S(2)}) copy-start(f32[16,8192]{1,0:T(8,128)S(1)} %get-tuple-element.62) | copy-start | bytes 1572868
  145.7 60.9 %copy-start.26 = (f32[16,8192]{1,0:T(8,128)S(1)}, f32[16,8192]{1,0:T(8,128)}, u32[]{:S(2)}) copy-start(f32[16,8192]{1,0:T(8,128)} %get-tuple-element.86) | copy-start | bytes 1572868
  213.3 60.5 %copy-start.14 = (f32[16,8192]{1,0:T(8,128)S(1)}, f32[16,8192]{1,0:T(8,128)}, u32[]{:S(2)}) copy-start(f32[16,8192]{1,0:T(8,128)} %copy-done.13) | copy-start | bytes 1572868
  282.6 61.0 %copy-start.4 = (f32[16,8192]{1,0:T(8,128)S(1)}, f32[16,8192]{1,0:T(8,128)}, u32[]{:S(2)}) copy-start(f32[16,8192]{1,0:T(8,128)} %get-tuple-element.55) | copy-start | bytes 1572868
  481.7 18.2 %slice-start.4 = ((s8[8388608]{0:T(1024)(128)(4,1)}), s8[4194304]{0:T(1024)(128)(4,1)S(1)}, s32[]{:S(2)}) async-start(s8[8388608]{0:T(1024)(128)(4,1)} %bitcast.264), calls=%async_computation.9 | async-start | bytes 8388608
  489.1 5.4 copy-start.8
  489.1 5.4 copy-start.1
  489.1 10.8 slice-start.5
  494.5 7.2 slice-start
  499.9 2.2 slice-start.1
  499.9 2.3 copy-start.6
  505.8 1.8 copy-start.5
  511.3 1.8 copy-start.3
  514.9 1.8 copy-start.39
  514.9 57.8 %copy-start.7 = (f32[16,8192]{1,0:T(8,128)S(1)}, f32[16,8192]{1,0:T(8,128)}, u32[]{:S(2)}) copy-start(f32[16,8192]{1,0:T(8,128)} %get-tuple-element.48) | copy-start | bytes 1572868
  514.9 57.8 %copy-start.9 = (f32[16,8192]{1,0:T(8,128)S(1)}, f32[16,8192]{1,0:T(8,128)}, u32[]{:S(2)}) copy-start(f32[16,8192]{1,0:T(8,128)} %copy-done.8) | copy-start | bytes 1572868
  514.9 57.8 %copy-start.12 = (f32[16,8192]{1,0:T(8,128)S(1)}, f32[16,8192]{1,0:T(8,128)}, u32[]{:S(2)}) copy-start(f32[16,8192]{1,0:T(8,128)} %get-tuple-element.50) | copy-start | bytes 1572868
  579.3 9.5 slice-start.2
  584.0 4.7 slice-start.3
  584.1 4.7 copy-start.22
  588.8 1.2 copy-start.21
  590.0 1.2 copy-start.20
  592.4 1.3 copy-start.29
  592.4 1.3 copy-start.30
  592.4 1.3 copy-start.31
  592.4 1.3 copy-start.32
  592.4 1.3 copy-start.33
  592.4 1.3 copy-start.34
  592.5 1.3 copy-start.35
  592.5 1.3 copy-start.36
  592.5 1.3 copy-start.37
  592.5 1.3 copy-start.38
  592.5 63.6 %copy-start.19 = (bf16[8,16,8192]{2,1,0:T(8,128)(2,1)S(1)}, bf16[8,16,8192]{2,1,0:T(8,128)(2,1)}, u32[]{:S(2)}) copy-start(bf16[8,16,8192]{2,1,0:T(8,128)(2,1)} %get-tuple-element.42) | copy-start | bytes 6291460
  688.8 165.1 %all-to-all-start.1 = ((bf16[8,2,65536]{2,1,0:T(2,128)(2,1)}), bf16[8,2,65536]{2,1,0:T(2,128)(2,1)S(1)}, u32[]{:S(2)}, u32[]{:S(2)}) async-start(bf16[8,2,65536]{2,1,0:T(2,128)(2,1)} %reshape.114), calls=%async_computation.1 | async-start | bytes 4194304 | tf_op jit(solution)/shard_map/all_to_all | solution.py:81
  817.1 111.2 %all-gather.3.cloned.1.call-start = ((), (), s32[]{:S(2)}) async-start(), calls=%async_computation.2 | async-start | bytes 1179648 | tf_op jit(solution)/shard_map/all_gather | solution.py:85
  853.9 42.9 %all-to-all-start = ((bf16[8,2,65536]{2,1,0:T(2,128)(2,1)}), bf16[8,2,65536]{2,1,0:T(2,128)(2,1)}, u32[]{:S(2)}, u32[]{:S(2)}) async-start(bf16[8,2,65536]{2,1,0:T(2,128)(2,1)} %reshape.112), calls=%async_computation | async-start | bytes 4194304 | tf_op jit(solution)/shard_map/all_to_all | solution.py:80
  858.7 183.2 %all-reduce.5.cloned.1.call-start = ((), (), s32[]{:S(2)}) async-start(), calls=%async_computation.4 | async-start | bytes 2097152 | tf_op jit(solution)/shard_map/psum | solution.py:99
  1041.9 2.6 copy-start.15
  (3 other events, 2.3 us)
Sparse Core Ops, SparseCore 0:
  656.3 144.7 all-gather.4
  819.6 23.4 all-gather.2
  897.0 144.9 all-reduce.4
where the time goes:
time: 1230 us; the launch traced here: 1210 us
  blocking collectives  516 us (42%)
  matrix products  162 us (13%)
  local copies, waits for them, and re-layouts  149 us (12%)
  starting transfers between devices  133 us (11%)
  other arithmetic  127 us (10%)
  waiting for transfers between devices  109 us (9%)
  between operations  17.4 us (1%)
    psum x8, blocking collectives, shards(): projected = lax.psum(partial_value, 'neuron').astype(jnp.bfloat16)  455 us
    all_to_all x1, starting transfers between devices, shards(): lax.all_to_all(presyn_all, 'trial', split_axis=2, concat_axis=1, tiled=True)  128 us
    psum x1, waiting for transfers between devices, shards(): lax.psum(lax.dot_general(right_step, right_step, row_lead, precision=high...  109 us
    another operation x14, other arithmetic, shards(): lower_one = jnp.linalg.cholesky(gram_one)  78.7 us
    dot_general x24, matrix products, rank_block(): return jnp.dot(values, factor, preferred_element_type=jnp.float32) * weight  71.5 us
    unnamed x111, local copies, waits for them, and re-layouts  70.7 us
    psum x1, blocking collectives, shards(): g_total, k_total = lax.psum((g_part, k_part), 'neuron')  61.6 us
    dot_general x8, matrix products, shards(): lax.dot_general(projected, left_factor, (((1,), (1,)), ((), ())), preferr...  55.8 us
  transfers between devices with their start and end apart: 5, of which 1 were waited for; matrix products, arithmetic and copies ran while one was open for 12% of the time, Pallas kernels for 0%

commit v1 on v0

--- a/solution.py
+++ b/solution.py
@@ -6,6 +6,13 @@
 
 sharpness = 3.0
 learn_rate = 0.5
+
+
+def exchange_blocks(x, name, split, join):
+    size = lax.axis_size(name)
+    pieces = jnp.stack(jnp.split(x, size, axis=split), axis=0)
+    pieces = lax.all_to_all(pieces, name, split_axis=0, concat_axis=0)
+    return jnp.concatenate(pieces, axis=join)
 
 
 def rank_block(values, factor, weight):
@@ -78,7 +85,7 @@
     contract_lead = (((0, 1), (0, 1)), ((), ()))
     signal_mine, presyn_mine = (
         lax.all_to_all(signal_all, "trial", split_axis=2, concat_axis=1, tiled=True),
-        lax.all_to_all(presyn_all, "trial", split_axis=2, concat_axis=1, tiled=True),
+        exchange_blocks(presyn_all, "trial", 2, 1),
     )
     first = lax.dot_general(
         signal_mine,

time: 1230 us -> 1190 us (0.967)
  local copies, waits for them, and re-layouts: 149 us -> 99.6 us
  matrix products: 162 us -> 176 us
    unnamed x111 -> x120, local copies, waits for them, and re-layouts: 70.7 us -> 46.5 us
    all_to_all x1 -> x0, local copies, waits for them, and re-layouts: 17.1 us -> none  [shards(): lax.all_to_all(presyn_all, 'trial', split_axis=2, concat_axis=1, tiled=True)]
    all_to_all x1, waiting for transfers between devices: 0.01 us -> 15.7 us  [shards(): lax.all_to_all(signal_all, 'trial', split_axis=2, concat_axis=1, tiled=True)]
    dot_general x24, matrix products: 71.5 us -> 86.7 us  [rank_block(): return jnp.dot(values, factor, preferred_element_type=jnp.float32) * weight]
    psum x1, waiting for transfers between devices: 109 us -> 96 us  [shards(): lax.psum(lax.dot_general(right_step, right_step, row_lead, precision=high...]
  transfers between devices with their start and end apart: 5 -> 5, of which waited for: 1 -> 2; matrix products, arithmetic and copies ran while one was open for 12% -> 8% of each run, Pallas kernels for 0% -> 0%
where the time goes in v1:
time: 1190 us; the launch traced here: 1180 us
  blocking collectives  514 us (43%)
  matrix products  176 us (15%)
  starting transfers between devices  135 us (11%)
  other arithmetic  126 us (11%)
  waiting for transfers between devices  112 us (9%)
  local copies, waits for them, and re-layouts  99.6 us (8%)
  between operations  17.4 us (1%)
    psum x8, blocking collectives, shards(): projected = lax.psum(partial_value, 'neuron').astype(jnp.bfloat16)  453 us
    all_to_all x1, starting transfers between devices, exchange_blocks(): pieces = lax.all_to_all(pieces, name, split_axis=0, concat_axis=0)  130 us
    psum x1, waiting for transfers between devices, shards(): lax.psum(lax.dot_general(right_step, right_step, row_lead, precision=high...  96 us
    dot_general x24, matrix products, rank_block(): return jnp.dot(values, factor, preferred_element_type=jnp.float32) * weight  86.7 us
    another operation x14, other arithmetic, shards(): lower_one = jnp.linalg.cholesky(gram_one)  79.1 us
    psum x1, blocking collectives, shards(): g_total, k_total = lax.psum((g_part, k_part), 'neuron')  61.3 us
    dot_general x8, matrix products, shards(): lax.dot_general(projected, left_factor, (((1,), (1,)), ((), ())), preferr...  54.6 us
    unnamed x120, local copies, waits for them, and re-layouts  46.5 us
  transfers between devices with their start and end apart: 5, of which 2 were waited for; matrix products, arithmetic and copies ran while one was open for 8% of the time, Pallas kernels for 0%

profile of v1, /device:TPU:1, one launch (start us, length us, event | category | flops | bytes accessed | tf_op | source)
XLA Modules:
  0.0 1180.8 jit_solution(11981548736725691954)
XLA Ops:
  7.3 5.0 convolution_multiply_fusion.31
  12.3 62.5 %psum.175 = bf16[16,512]{1,0:T(8,128)(2,1)S(1)} all-reduce(f32[16,512]{1,0:T(8,128)S(1)} %convolution_multiply_fusion.31), channel_id=1, replica_groups=mesh['neuron'=16,'trial'=8] {'neuron'}, use_global_device_ids=true, to_apply=%region_0.0 | all-reduce | flops 8192 | bytes 49152 | tf_op jit(solution)/shard_map/psum | solution.py:51
  74.9 6.7 bitcast_dynamic-update-slice_fusion.8
  82.8 55.9 %psum.176 = bf16[16,512]{1,0:T(8,128)(2,1)S(1)} all-reduce(f32[16,512]{1,0:T(8,128)S(1)} %convolution_multiply_fusion.30), channel_id=1, replica_groups=mesh['neuron'=16,'trial'=8] {'neuron'}, use_global_device_ids=true, to_apply=%region_1.0 | all-reduce | flops 8192 | bytes 49152 | tf_op jit(solution)/shard_map/psum | solution.py:51
  138.7 5.4 convolution_multiply_fusion.15
  144.1 7.0 bitcast_dynamic-update-slice_fusion.7
  156.9 55.6 %psum.177 = bf16[16,512]{1,0:T(8,128)(2,1)S(1)} all-reduce(f32[16,512]{1,0:T(8,128)S(1)} %convolution_multiply_fusion.29), channel_id=1, replica_groups=mesh['neuron'=16,'trial'=8] {'neuron'}, use_global_device_ids=true, to_apply=%region_2.0 | all-reduce | flops 8192 | bytes 49152 | tf_op jit(solution)/shard_map/psum | solution.py:51
  212.5 6.6 bitcast_dynamic-update-slice_fusion.6
  219.2 5.3 convolution_multiply_fusion.13
  224.5 4.6 convolution_multiply_fusion.28
  229.0 56.0 %psum.178 = bf16[16,512]{1,0:T(8,128)(2,1)S(1)} all-reduce(f32[16,512]{1,0:T(8,128)S(1)} %convolution_multiply_fusion.28), channel_id=1, replica_groups=mesh['neuron'=16,'trial'=8] {'neuron'}, use_global_device_ids=true, to_apply=%region_3.0 | all-reduce | flops 8192 | bytes 49152 | tf_op jit(solution)/shard_map/psum | solution.py:51
  285.0 7.0 bitcast_dynamic-update-slice_fusion.5
  292.0 4.8 convolution_multiply_fusion.27
  296.8 5.4 convolution_multiply_fusion.12
  304.1 55.6 %psum.179 = bf16[16,512]{1,0:T(8,128)(2,1)S(1)} all-reduce(f32[16,512]{1,0:T(8,128)S(1)} %convolution_multiply_fusion.27), channel_id=1, replica_groups=mesh['neuron'=16,'trial'=8] {'neuron'}, use_global_device_ids=true, to_apply=%region_4.0 | all-reduce | flops 8192 | bytes 49152 | tf_op jit(solution)/shard_map/psum | solution.py:51
  359.7 6.6 bitcast_dynamic-update-slice_fusion.4
  366.4 5.3 convolution_multiply_fusion.11
  376.2 55.7 %psum.180 = bf16[16,512]{1,0:T(8,128)(2,1)S(1)} all-reduce(f32[16,512]{1,0:T(8,128)S(1)} %convolution_multiply_fusion.26), channel_id=1, replica_groups=mesh['neuron'=16,'trial'=8] {'neuron'}, use_global_device_ids=true, to_apply=%region_5.0 | all-reduce | flops 8192 | bytes 49152 | tf_op jit(solution)/shard_map/psum | solution.py:51
  433.6 7.0 bitcast_dynamic-update-slice_fusion.3
  440.7 4.8 convolution_multiply_fusion.25
  445.5 5.4 convolution_multiply_fusion.10
  452.7 56.0 %psum.181 = bf16[16,512]{1,0:T(8,128)(2,1)S(1)} all-reduce(f32[16,512]{1,0:T(8,128)S(1)} %convolution_multiply_fusion.25), channel_id=1, replica_groups=mesh['neuron'=16,'trial'=8] {'neuron'}, use_global_device_ids=true, to_apply=%region_6.0 | all-reduce | flops 8192 | bytes 49152 | tf_op jit(solution)/shard_map/psum | solution.py:51
  510.5 6.7 bitcast_dynamic-update-slice_fusion.2
  517.2 5.4 convolution_multiply_fusion.24
  522.7 5.3 convolution_multiply_fusion.9
  533.4 55.7 %psum.182 = bf16[16,512]{1,0:T(8,128)(2,1)S(1)} all-reduce(f32[16,512]{1,0:T(8,128)S(1)} %copy-done.37), channel_id=1, replica_groups=mesh['neuron'=16,'trial'=8] {'neuron'}, use_global_device_ids=true, to_apply=%region_7.0 | all-reduce | flops 8192 | bytes 49152 | tf_op jit(solution)/shard_map/psum | solution.py:51
  589.2 6.8 bitcast_dynamic-update-slice_fusion.1
  596.0 4.8 convolution_multiply_fusion.16
  600.9 4.6 convolution_multiply_fusion.8
  605.6 61.3 %all-reduce.6 = (bf16[16,512]{1,0:T(8,128)(2,1)S(1)}, bf16[16,512]{1,0:T(8,128)(2,1)S(1)}, bf16[16,512]{1,0:T(8,128)(2,1)S(1)}, bf16[16,512]{1,0:T(8,128)(2,1)S(...) all-reduce(f32[16,512]{1,0:T(8,128)S(1)} %copy-done.36, ...), channel_id=1, replica_groups=mesh['neuron'=16,'trial'=8] {'neuron'}, use_global_device_ids=true, to_apply=%region_8.0 | all-reduce | flops 131072 | bytes 786432 | tf_op jit(solution)/shard_map/psum | solution.py:74
  677.5 129.9 %all-to-all-start.1 = ((bf16[8,8,16,1024]{3,2,1,0:T(8,128)(2,1)}), bf16[8,8,16,1024]{3,2,1,0:T(8,128)(2,1)}, u32[]{:S(2)}, u32[]{:S(2)}) async-start(bf16[8,8,16,1024]{3,2,1,0:T(8,128)(2,1)} %fusion.61), calls=%async_computation.1 | async-start | bytes 4194304 | tf_op jit(solution)/shard_map/all_to_all | solution.py:14
  809.3 14.5 %copy.29 = bf16[8,16,8192]{1,0,2:T(8,128)(2,1)} copy(bf16[8,16,8192]{2,1,0:T(8,128)(2,1)} %bitcast_dynamic-update-slice_fusion.9) | data formatting | bytes 4194304 | tf_op jit(solution)/shard_map/stack | solution.py:77
  823.9 19.6 %reshape.120 = bf16[8,2,65536]{2,1,0:T(2,128)(2,1)} reshape(bf16[8192,8,16]{2,1,0:T(8,128)(2,1)} %bitcast.297) | data formatting | bytes 4194304
  843.5 4.8 all-to-all-start
  859.5 15.7 %all-to-all-done = bf16[8,2,65536]{2,1,0:T(2,128)(2,1)} async-done(((bf16[8,2,65536]{2,1,0:T(2,128)(2,1)}), bf16[8,2,65536]{2,1,0:T(2,128)(2,1)}, u32[]{:S(2)}, u32[]{:S(2)}) %all-to-all-start) | async-done | bytes 2097184 | tf_op jit(solution)/shard_map/all_to_all | solution.py:87
  875.2 13.9 %reshape.121 = bf16[8192,8,16]{2,1,0:T(8,128)(2,1)} reshape(bf16[8,2,65536]{2,1,0:T(2,128)(2,1)} %all-to-all-done) | data formatting | bytes 4194304
  889.1 17.2 %copy.31 = bf16[8,8,16,1024]{3,2,1,0:T(8,128)(2,1)} copy(bf16[8,8,16,1024]{2,0,3,1:T(8,128)(2,1)} %bitcast.298) | data formatting | bytes 4194304 | tf_op jit(solution)/shard_map/all_to_all | solution.py:87
  910.9 96.0 %all-reduce.5.cloned.1.call-done = f32[512,512]{0,1:T(8,128)} async-done(((f32[512,512]{0,1:T(8,128)}), f32[512,512]{0,1:T(8,128)}) %all-reduce.5.cloned.1.call-update) | async-done | bytes 1048592 | tf_op jit(solution)/shard_map/psum | solution.py:106
  1011.9 11.7 cholesky.104
  1023.6 9.8 custom-call.30
  1036.1 11.7 cholesky.217
  1047.8 10.0 custom-call.31
  1059.4 11.7 cholesky.238
  1071.8 9.8 custom-call.32
  1083.1 12.1 %cholesky.255 = f32[128,128]{1,0:T(8,128)S(1)} custom-call(f32[128,128]{1,0:T(8,128)S(1)} %convolution_subtract_fusion.4), custom_call_target="Cholesky" | custom-call | tf_op jit(solution)/shard_map/jit(cholesky)/cholesky | solution.py:109
  1100.5 14.6 %while.1 = (s32[]{:T(128)}, f32[512,512]{1,0:T(8,128)}, s32[4,2]{0,1:T(2,128)S(1)}, f32[4,128,128]{2,1,0:T(8,128)}, s32[]{:T(128)}) while((s32[]{:T(128)}, f32[512,512]{1,0:T(8,128)}, s32[4,2]{0,1:T(2,128)S(1)}, f32[4,128,128]{2,1,0:T(8,128)}, s32[]{:T(128)}) %tuple.66), condition=%wide.while_cond, body=%wide.while_body.sunk | while | flops 2 | bytes 132205 | solution.py:110
  1115.1 40.1 %custom-call.33 = f32[4,128,128]{1,2,0:T(8,128)S(1)} custom-call(f32[4,128,128]{2,1,0:T(8,128)} %get-tuple-element.9), custom_call_target="InvertDiagBlocksLowerTriangular" | custom-call | tf_op jit(solution)/shard_map/triangular_solve | solution.py:110
  1167.7 6.4 multiply_convert_fusion
  (196 shorter events, 93.4 us)
Async XLA Ops:
  7.2 67.7 %copy-start.13 = (f32[8192]{0:T(1024)S(1)}, f32[8192]{0:T(1024)}, u32[]{:S(2)}) copy-start(f32[8192]{0:T(1024)} %param.19) | copy-start | bytes 98308
  7.2 67.7 %copy-start.12 = (f32[8192]{0:T(1024)S(1)}, f32[8192]{0:T(1024)}, u32[]{:S(2)}) copy-start(f32[8192]{0:T(1024)} %param.18) | copy-start | bytes 98308
  7.2 67.7 %copy-start.3 = (f32[16,8192]{1,0:T(8,128)S(1)}, f32[16,8192]{1,0:T(8,128)}, u32[]{:S(2)}) copy-start(f32[16,8192]{1,0:T(8,128)} %param.14) | copy-start | bytes 1572868
  7.2 67.7 %copy-start.4 = (f32[16,8192]{1,0:T(8,128)S(1)}, f32[16,8192]{1,0:T(8,128)}, u32[]{:S(2)}) copy-start(f32[16,8192]{1,0:T(8,128)} %param.13) | copy-start | bytes 1572868
  7.2 67.7 %copy-start.18 = (f32[8192]{0:T(1024)S(1)}, f32[8192]{0:T(1024)}, u32[]{:S(2)}) copy-start(f32[8192]{0:T(1024)} %param.17) | copy-start | bytes 98308
  7.2 67.7 %copy-start.17 = (f32[8192]{0:T(1024)S(1)}, f32[8192]{0:T(1024)}, u32[]{:S(2)}) copy-start(f32[8192]{0:T(1024)} %param.16) | copy-start | bytes 98308
  7.2 67.7 %copy-start.19 = (f32[16,8192]{1,0:T(8,128)S(1)}, f32[16,8192]{1,0:T(8,128)}, u32[]{:S(2)}) copy-start(f32[16,8192]{1,0:T(8,128)} %param.15) | copy-start | bytes 1572868
  7.2 844.3 %all-gather.5.cloned.1.call-start = ((), (), s32[]{:S(2)}) async-start(), calls=%async_computation.3 | async-start | bytes 1179648 | tf_op jit(solution)/shard_map/all_gather | solution.py:98
  74.9 6.7 copy-start
  138.7 5.4 copy-start.20
  138.7 12.5 %slice-start = ((s8[8388608]{0:T(1024)(128)(4,1)}), s8[4194304]{0:T(1024)(128)(4,1)S(1)}, s32[]{:S(2)}) async-start(s8[8388608]{0:T(1024)(128)(4,1)} %bitcast.287), calls=%async_computation.5 | async-start | bytes 8388608
  138.7 13.7 %slice-start.8 = ((s8[8388608]{0:T(1024)(128)(4,1)}), s8[4194304]{0:T(1024)(128)(4,1)S(1)}, s32[]{:S(2)}) async-start(s8[8388608]{0:T(1024)(128)(4,1)} %bitcast.295), calls=%async_computation.13 | async-start | bytes 8388608
  144.1 7.0 slice-start.1
  144.1 8.2 slice-start.9
  151.1 61.4 %copy-start.7 = (f32[16,8192]{1,0:T(8,128)}, f32[16,8192]{1,0:T(8,128)S(1)}, u32[]{:S(2)}) copy-start(f32[16,8192]{1,0:T(8,128)S(1)} %get-tuple-element.64) | copy-start | bytes 1572868
  155.1 57.4 %copy-start.23 = (f32[16,8192]{1,0:T(8,128)S(1)}, f32[16,8192]{1,0:T(8,128)}, u32[]{:S(2)}) copy-start(f32[16,8192]{1,0:T(8,128)} %get-tuple-element.86) | copy-start | bytes 1572868
  292.0 67.7 %copy-start.6 = (f32[16,8192]{1,0:T(8,128)}, f32[16,8192]{1,0:T(8,128)S(1)}, u32[]{:S(2)}) copy-start(f32[16,8192]{1,0:T(8,128)S(1)} %get-tuple-element.57) | copy-start | bytes 1572868
  292.0 10.2 slice-start.2
  296.8 5.4 slice-start.3
  302.3 57.4 %copy-start.22 = (f32[16,8192]{1,0:T(8,128)S(1)}, f32[16,8192]{1,0:T(8,128)}, u32[]{:S(2)}) copy-start(f32[16,8192]{1,0:T(8,128)} %get-tuple-element.88) | copy-start | bytes 1572868
  440.7 69.8 %copy-start.5 = (f32[16,8192]{1,0:T(8,128)}, f32[16,8192]{1,0:T(8,128)S(1)}, u32[]{:S(2)}) copy-start(f32[16,8192]{1,0:T(8,128)S(1)} %get-tuple-element.50) | copy-start | bytes 1572868
  440.7 10.2 slice-start.4
  445.5 5.4 slice-start.5
  450.9 59.6 %copy-start.21 = (f32[16,8192]{1,0:T(8,128)S(1)}, f32[16,8192]{1,0:T(8,128)}, u32[]{:S(2)}) copy-start(f32[16,8192]{1,0:T(8,128)} %get-tuple-element.90) | copy-start | bytes 1572868
  517.2 5.4 copy-start.2
  517.2 5.4 copy-start.1
  517.2 10.8 slice-start.6
  522.7 5.3 slice-start.7
  528.0 1.8 copy-start.15
  596.0 4.8 copy-start.8
  600.8 4.8 copy-start.26
  600.8 4.8 copy-start.27
  600.8 4.7 copy-start.28
  600.8 4.7 copy-start.29
  600.8 4.7 copy-start.30
  600.8 4.7 copy-start.31
  600.8 4.7 copy-start.32
  600.8 4.7 copy-start.33
  600.8 4.7 copy-start.34
  600.9 4.7 copy-start.35
  600.9 4.7 copy-start.36
  667.7 6.9 copy-start.14
  677.5 131.1 %copy-start.9 = (f32[16,8192]{1,0:T(8,128)S(1)}, f32[16,8192]{1,0:T(8,128)}, u32[]{:S(2)}) copy-start(f32[16,8192]{1,0:T(8,128)} %copy-done.8) | copy-start | bytes 1572868
  677.5 166.0 %all-to-all-start.1 = ((bf16[8,8,16,1024]{3,2,1,0:T(8,128)(2,1)}), bf16[8,8,16,1024]{3,2,1,0:T(8,128)(2,1)}, u32[]{:S(2)}, u32[]{:S(2)}) async-start(bf16[8,8,16,1024]{3,2,1,0:T(8,128)(2,1)} %fusion.61), calls=%async_computation.1 | async-start | bytes 4194304 | tf_op jit(solution)/shard_map/all_to_all | solution.py:14
  807.4 99.0 %all-gather.3.cloned.1.call-start = ((), (), s32[]{:S(2)}) async-start(), calls=%async_computation.2 | async-start | bytes 1179648 | tf_op jit(solution)/shard_map/all_gather | solution.py:92
  843.5 31.8 %all-to-all-start = ((bf16[8,2,65536]{2,1,0:T(2,128)(2,1)}), bf16[8,2,65536]{2,1,0:T(2,128)(2,1)}, u32[]{:S(2)}, u32[]{:S(2)}) async-start(bf16[8,2,65536]{2,1,0:T(2,128)(2,1)} %reshape.120), calls=%async_computation | async-start | bytes 4194304 | tf_op jit(solution)/shard_map/all_to_all | solution.py:87
  848.2 158.6 %all-reduce.5.cloned.1.call-start = ((), (), s32[]{:S(2)}) async-start(), calls=%async_computation.4 | async-start | bytes 2097152 | tf_op jit(solution)/shard_map/psum | solution.py:106
  1006.8 2.6 copy-start.10
  (5 other events, 4.7 us)
Sparse Core Ops, SparseCore 0:
  667.8 149.1 all-gather.4
  818.7 25.6 all-gather.2
  859.6 147.1 all-reduce.4
